TPU v7x, 512 devices: a whole 4x4x16 slice. The times are simulated.
512 devices in a mesh: fib: 16 (over y, x), blk: 32 (over z, core).
Axes of the slice: x: 4, y: 4, z: 16, core: 2. Of those that a mesh axis runs over, the one named last changes fastest.
Arguments:
- field_data: float32 [33, 64, 512, 256], P(None, 'blk', 'fib'), may hold values from -120 to 120
- start_block: float32 [512, 64], replicated, may hold values from -6 to 6
Outputs:
- core_out: float32 [33, 64, 64, 256], P(None, 'blk', 'fib')
All inputs are finite; a program needn't handle non-finite values.
Results may differ from a plain program's by a relative error of at most 0.00013.
Values sent between devices are 32-bit elements; how exact they have to be, the bound alone decides.
A program may use at most 192 MiB of HBM per device.

v0:
```python
import jax
import jax.numpy as jnp
from jax import lax
from jax.sharding import PartitionSpec as P


def shards(field_data, start_block):
    highest = lax.Precision.HIGHEST
    received = lax.all_to_all(field_data, "fib", split_axis=3, concat_axis=2, tiled=True)
    width_x = received.shape[2]
    unfolded = jnp.transpose(received, (0, 1, 3, 2)).reshape(-1, width_x)
    contract_rows = (((0,), (0,)), ((), ()))
    local_gram = lax.dot_general(unfolded, unfolded, contract_rows, precision=highest)
    gram_total = lax.psum(local_gram, ("fib", "blk"))
    raw_basis = jnp.dot(gram_total, start_block, precision=highest)
    inner_block = jnp.dot(raw_basis.T, raw_basis, precision=highest)
    lower_factor = jnp.linalg.cholesky(inner_block)
    basis_cols = jax.scipy.linalg.solve_triangular(lower_factor, raw_basis.T, lower=True).T
    core_local = jnp.einsum("szxy,xr->szry", received, basis_cols, precision=highest)
    return lax.all_to_all(core_local, "fib", split_axis=2, concat_axis=3, tiled=True)


def solution(mesh):
    in_specs = (P(None, "blk", "fib", None), P())
    out_specs = P(None, "blk", "fib", None)
    return jax.shard_map(shards, mesh=mesh, in_specs=in_specs, out_specs=out_specs, check_vma=False)
```

profile of v0, /device:TPU:1, one launch (start us, length us, event | category | flops | bytes accessed | tf_op | source)
XLA Modules:
  0.0 619.4 jit_solution(7491580162648552195)
XLA Ops:
  6.5 0.0 copy-start
  6.5 0.0 all-reduce.2.cloned.1.call-start
  6.5 8.7 %copy.13 = f32[33,2,32,256]{0,2,1,3:T(8,128)} copy(f32[33,2,32,256]{3,2,1,0:T(8,128)} %param.2) | data formatting | bytes 4325376 | tf_op args[0]
  15.2 10.1 %reshape.13 = f32[16,1,33792]{2,1,0:T(1,128)S(1)} reshape(f32[256,2,32,33]{3,2,1,0:T(8,128)} %bitcast.45) | data formatting | bytes 4325376
  25.3 34.1 %all_to_all.36 = f32[16,1,33792]{2,1,0:T(1,128)} all-to-all(f32[16,1,33792]{2,1,0:T(1,128)S(1)} %reshape.13), channel_id=1, replica_groups=mesh['fib'=16,'blk'=32] {'fib'}, dimensions={0} | all-to-all | bytes 4325376 | tf_op jit(solution)/shard_map/all_to_all | solution.py:9
  59.4 0.5 broadcast.53
  59.9 7.4 %reduce.6 = f32[16,33792]{1,0:T(8,128)S(1)} reduce(f32[16,1,33792]{2,1,0:T(1,128)} %all_to_all.36, f32[]{:T(128)} %broadcast.53), dimensions={1}, to_apply=%all_to_all.26.reduce_sub_computation | reduce | bytes 4325380 | tf_op jit(solution)/shard_map/all_to_all | solution.py:9
  67.3 12.4 %reshape.14 = f32[256,2,32,33]{3,2,1,0:T(8,128)} reshape(f32[16,33792]{1,0:T(8,128)S(1)} %reduce.6) | data formatting | bytes 4325376
  79.8 11.7 %copy.15 = f32[33,2,16,32,16]{3,2,4,1,0:T(8,128)} copy(f32[33,2,16,32,16]{0,3,1,4,2:T(8,128)} %bitcast.46) | data formatting | bytes 4325376 | tf_op jit(solution)/shard_map/all_to_all | solution.py:9
  91.5 6.7 %all_to_all.29 = f32[33,2,512,16]{2,3,1,0:T(8,128)S(1)} reshape(f32[33,2,16,32,16]{3,2,4,1,0:T(8,128)} %copy.15) | data formatting | bytes 4325376 | tf_op jit(solution)/shard_map/all_to_all | solution.py:9
  98.2 5.4 fusion.4
  103.5 0.0 all-reduce.2.cloned.1.call-update
  103.6 470.4 %all-reduce.2.cloned.1.call-done = f32[512,512]{1,0:T(8,128)} async-done(((f32[512,512]{1,0:T(8,128)}), f32[512,512]{1,0:T(8,128)}) %all-reduce.2.cloned.1.call-update) | async-done | bytes 1048592 | tf_op jit(solution)/shard_map/psum | solution.py:14
  574.0 0.0 copy-done
  574.0 2.4 fusion.13
  576.4 0.3 fusion.14
  576.6 0.1 copy.16
  576.7 5.8 cholesky.16
  582.6 0.7 compare_reduce_fusion
  583.3 0.7 fusion.10
  584.0 4.9 custom-call.7
  588.9 0.3 convolution_bitcast_fusion
  589.3 3.0 fusion.7
  592.3 1.0 copy.18
  593.3 1.0 reshape.15
  594.3 14.6 %all_to_all.37 = f32[16,1,4224]{2,1,0:T(1,128)S(1)} all-to-all(f32[16,1,4224]{2,1,0:T(1,128)S(1)} %reshape.15), channel_id=1, replica_groups=mesh['fib'=16,'blk'=32] {'fib'}, dimensions={0} | all-to-all | bytes 540672 | tf_op jit(solution)/shard_map/all_to_all | solution.py:20
  608.9 1.3 reduce.7
  610.2 1.1 reshape.16
  611.4 0.1 copy.20
  611.5 1.0 copy.21
  (2 shorter events, 0.0 us)
Async XLA Ops:
  6.5 567.5 %copy-start = (f32[512,64]{0,1:T(8,128)S(1)}, f32[512,64]{0,1:T(8,128)}, u32[]{:S(2)}) copy-start(f32[512,64]{0,1:T(8,128)} %param.3) | copy-start | bytes 393220
  6.5 567.5 %all-reduce.2.cloned.1.call-start = ((), (), s32[]{:S(2)}) async-start(), calls=%async_computation.2 | async-start | bytes 2097152 | tf_op jit(solution)/shard_map/psum | solution.py:14
Sparse Core Ops, SparseCore 0:
  103.7 470.2 all-reduce.1
where the time goes:
time: 620 us; the launch traced here: 619 us
  waiting for transfers between devices  470 us (76%)
  local copies, waits for them, and re-layouts  54.5 us (9%)
  blocking collectives  48.7 us (8%)
  other arithmetic  20.9 us (3%)
  between operations  13.5 us (2%)
  matrix products  11.3 us (2%)
    psum x1, waiting for transfers between devices, shards(): gram_total = lax.psum(local_gram, ('fib', 'blk'))  470 us
    all_to_all x1, blocking collectives, shards(): lax.all_to_all(field_data, 'fib', split_axis=3, concat_axis=2, tiled=True)  34.1 us
    unnamed x7, local copies, waits for them, and re-layouts  33.4 us
    all_to_all x3, local copies, waits for them, and re-layouts, shards(): lax.all_to_all(field_data, 'fib', split_axis=3, concat_axis=2, tiled=True)  18.9 us
    all_to_all x1, blocking collectives, shards(): lax.all_to_all(core_local, 'fib', split_axis=2, concat_axis=3, tiled=True)  14.6 us
  transfers between devices with their start and end apart: 1, of which 1 were waited for; matrix products, arithmetic and copies ran while one was open for 0% of the time, Pallas kernels for 0%

commit v1 on v0

--- a/solution.py
+++ b/solution.py
@@ -17,7 +17,10 @@
     lower_factor = jnp.linalg.cholesky(inner_block)
     basis_cols = jax.scipy.linalg.solve_triangular(lower_factor, raw_basis.T, lower=True).T
     core_local = jnp.einsum("szxy,xr->szry", received, basis_cols, precision=highest)
-    return lax.all_to_all(core_local, "fib", split_axis=2, concat_axis=3, tiled=True)
+    return jnp.concatenate(
+        lax.all_to_all(jnp.stack(jnp.split(core_local, lax.axis_size("fib"), axis=2)), "fib", 0, 0),
+        axis=3,
+    )
 
 
 def solution(mesh):

time: 620 us -> 650 us (1.048)
  local copies, waits for them, and re-layouts: 54.5 us -> 83.3 us
    another operation x0 -> x18, local copies, waits for them, and re-layouts: none -> 29.5 us  [shards(): jnp.stack(jnp.split(core_local, lax.axis_size('fib'), axis=2))]
    unnamed x7 -> x44, local copies, waits for them, and re-layouts: 33.4 us -> 33.5 us
where the time goes in v1:
time: 650 us; the launch traced here: 649 us
  waiting for transfers between devices  471 us (72%)
  local copies, waits for them, and re-layouts  83.3 us (13%)
  blocking collectives  48.7 us (7%)
  other arithmetic  20.8 us (3%)
  between operations  13.8 us (2%)
  matrix products  11.3 us (2%)
    psum x1, waiting for transfers between devices, shards(): gram_total = lax.psum(local_gram, ('fib', 'blk'))  471 us
    all_to_all x1, blocking collectives, shards(): lax.all_to_all(field_data, 'fib', split_axis=3, concat_axis=2, tiled=True)  34.1 us
    unnamed x44, local copies, waits for them, and re-layouts  33.5 us
    another operation x18, local copies, waits for them, and re-layouts, shards(): jnp.stack(jnp.split(core_local, lax.axis_size('fib'), axis=2))  29.5 us
    all_to_all x3, local copies, waits for them, and re-layouts, shards(): lax.all_to_all(field_data, 'fib', split_axis=3, concat_axis=2, tiled=True)  19 us
    all_to_all x1, blocking collectives, shards(): lax.all_to_all(jnp.stack(jnp.split(core_local, lax.axis_size('fib'), axis...  14.6 us
  transfers between devices with their start and end apart: 1, of which 1 were waited for; matrix products, arithmetic and copies ran while one was open for 0% of the time, Pallas kernels for 0%

profile of v1, /device:TPU:1, one launch (start us, length us, event | category | flops | bytes accessed | tf_op | source)
XLA Modules:
  0.0 648.6 jit_solution(9097699887688119448)
XLA Ops:
  6.5 0.0 copy-start
  6.5 8.7 %copy.11 = f32[33,2,32,256]{0,2,1,3:T(8,128)} copy(f32[33,2,32,256]{3,2,1,0:T(8,128)} %param.2) | data formatting | bytes 4325376 | tf_op args[0]
  15.2 10.1 %reshape.21 = f32[16,1,33792]{2,1,0:T(1,128)S(1)} reshape(f32[256,2,32,33]{3,2,1,0:T(8,128)} %bitcast.77) | data formatting | bytes 4325376
  25.3 34.1 %all_to_all.23 = f32[16,1,33792]{2,1,0:T(1,128)} all-to-all(f32[16,1,33792]{2,1,0:T(1,128)S(1)} %reshape.21), channel_id=1, replica_groups=mesh['fib'=16,'blk'=32] {'fib'}, dimensions={0} | all-to-all | bytes 4325376 | tf_op jit(solution)/shard_map/all_to_all | solution.py:9
  59.4 0.6 broadcast.53
  60.0 7.4 %reduce.6 = f32[16,33792]{1,0:T(8,128)S(1)} reduce(f32[16,1,33792]{2,1,0:T(1,128)} %all_to_all.23, f32[]{:T(128)} %broadcast.53), dimensions={1}, to_apply=%all_to_all.16.reduce_sub_computation | reduce | bytes 4325380 | tf_op jit(solution)/shard_map/all_to_all | solution.py:9
  67.4 12.4 %reshape.22 = f32[256,2,32,33]{3,2,1,0:T(8,128)} reshape(f32[16,33792]{1,0:T(8,128)S(1)} %reduce.6) | data formatting | bytes 4325376
  79.9 11.7 %copy.13 = f32[33,2,16,32,16]{3,2,4,1,0:T(8,128)} copy(f32[33,2,16,32,16]{0,3,1,4,2:T(8,128)} %bitcast.78) | data formatting | bytes 4325376 | tf_op jit(solution)/shard_map/all_to_all | solution.py:9
  91.6 6.7 %all_to_all.19 = f32[33,2,512,16]{2,3,1,0:T(8,128)S(1)} reshape(f32[33,2,16,32,16]{3,2,4,1,0:T(8,128)} %copy.13) | data formatting | bytes 4325376 | tf_op jit(solution)/shard_map/all_to_all | solution.py:9
  98.3 5.4 fusion.4
  103.6 0.0 all-reduce.2.cloned.1.call-update
  103.7 470.7 %all-reduce.2.cloned.1.call-done = f32[512,512]{1,0:T(8,128)} async-done(((f32[512,512]{1,0:T(8,128)}), f32[512,512]{1,0:T(8,128)}) %all-reduce.2.cloned.1.call-update) | async-done | bytes 1048592 | tf_op jit(solution)/shard_map/psum | solution.py:14
  574.3 0.0 copy-done
  574.3 2.4 fusion.13
  576.7 0.3 fusion.14
  577.0 0.1 copy.14
  577.0 5.8 cholesky.16
  582.9 0.6 compare_reduce_fusion
  583.6 0.7 fusion.10
  584.2 4.9 custom-call.7
  589.1 0.3 convolution_bitcast_fusion
  589.5 3.0 fusion.7
  592.5 5.7 slice_bitcast_fusion
  598.2 1.4 copy.31
  599.6 1.4 copy.30
  601.0 2.0 copy.29
  603.0 2.0 copy.28
  605.0 2.0 copy.27
  607.1 2.0 copy.26
  609.1 2.0 copy.25
  611.1 2.0 copy.24
  613.1 2.0 copy.23
  615.2 2.0 copy.22
  617.2 2.0 copy.21
  619.2 0.9 copy.20
  620.2 0.9 copy.19
  621.1 0.3 copy.18
  621.5 0.3 copy.17
  621.8 0.3 copy.16
  622.3 0.0 copy-done.6
  622.3 0.0 copy-done.5
  622.5 1.0 reshape.23
  623.5 14.6 %all_to_all.24 = f32[16,1,4224]{2,1,0:T(1,128)S(1)} all-to-all(f32[16,1,4224]{2,1,0:T(1,128)S(1)} %reshape.23), channel_id=1, replica_groups=mesh['fib'=16,'blk'=32] {'fib'}, dimensions={0} | all-to-all | bytes 540672 | tf_op jit(solution)/shard_map/all_to_all | solution.py:21
  638.1 1.3 reduce.7
  639.4 1.1 reshape.24
  640.5 0.1 bitcast_bitcast_fusion
  640.6 0.1 copy.32
  640.7 1.0 copy.33
  (39 shorter events, 0.2 us)
Async XLA Ops:
  6.5 567.8 %copy-start = (f32[512,64]{0,1:T(8,128)S(1)}, f32[512,64]{0,1:T(8,128)}, u32[]{:S(2)}) copy-start(f32[512,64]{0,1:T(8,128)} %param.3) | copy-start | bytes 393220
  6.5 567.8 %all-reduce.2.cloned.1.call-start = ((), (), s32[]{:S(2)}) async-start(), calls=%async_computation.2 | async-start | bytes 2097152 | tf_op jit(solution)/shard_map/psum | solution.py:14
  620.1 2.0 copy-start.10
  620.1 2.1 copy-start.9
  620.1 2.1 copy-start.8
  620.1 2.1 copy-start.7
  620.1 2.1 copy-start.6
  620.1 2.1 copy-start.5
  620.2 2.2 copy-start.4
  620.2 2.2 copy-start.3
  620.2 2.2 copy-start.2
  620.2 2.2 copy-start.1
  621.1 1.0 copy-start.11
Sparse Core Ops, SparseCore 0:
  103.8 470.5 all-reduce.1

commit v2 on v0

--- a/solution.py
+++ b/solution.py
@@ -11,7 +11,7 @@
     unfolded = jnp.transpose(received, (0, 1, 3, 2)).reshape(-1, width_x)
     contract_rows = (((0,), (0,)), ((), ()))
     local_gram = lax.dot_general(unfolded, unfolded, contract_rows, precision=highest)
-    gram_total = lax.psum(local_gram, ("fib", "blk"))
+    gram_total = lax.psum(lax.psum(local_gram, "fib"), "blk")
     raw_basis = jnp.dot(gram_total, start_block, precision=highest)
     inner_block = jnp.dot(raw_basis.T, raw_basis, precision=highest)
     lower_factor = jnp.linalg.cholesky(inner_block)

time: 620 us -> 483 us (0.78)
  waiting for transfers between devices: 470 us -> 333 us
    psum x1 -> x2, waiting for transfers between devices: 470 us -> 333 us  [shards(): gram_total = lax.psum(lax.psum(local_gram, 'fib'), 'blk')]
  transfers between devices with their start and end apart: 1 -> 2, of which waited for: 1 -> 2; matrix products, arithmetic and copies ran while one was open for 0% -> 0% of each run, Pallas kernels for 0% -> 0%
where the time goes in v2:
time: 483 us; the launch traced here: 482 us
  waiting for transfers between devices  333 us (69%)
  local copies, waits for them, and re-layouts  54.5 us (11%)
  blocking collectives  48.6 us (10%)
  other arithmetic  20.9 us (4%)
  between operations  13.5 us (3%)
  matrix products  11.3 us (2%)
    psum x2, waiting for transfers between devices, shards(): gram_total = lax.psum(lax.psum(local_gram, 'fib'), 'blk')  333 us
    all_to_all x1, blocking collectives, shards(): lax.all_to_all(field_data, 'fib', split_axis=3, concat_axis=2, tiled=True)  34.1 us
    unnamed x7, local copies, waits for them, and re-layouts  33.4 us
    all_to_all x3, local copies, waits for them, and re-layouts, shards(): lax.all_to_all(field_data, 'fib', split_axis=3, concat_axis=2, tiled=True)  18.9 us
    all_to_all x1, blocking collectives, shards(): lax.all_to_all(core_local, 'fib', split_axis=2, concat_axis=3, tiled=True)  14.5 us
  transfers between devices with their start and end apart: 2, of which 2 were waited for; matrix products, arithmetic and copies ran while one was open for 0% of the time, Pallas kernels for 0%

profile of v2, /device:TPU:1, one launch (start us, length us, event | category | flops | bytes accessed | tf_op | source)
XLA Modules:
  0.0 482.2 jit_solution(4122993338349420172)
XLA Ops:
  6.5 0.0 copy-start
  6.5 0.0 all-reduce.3.cloned.1.call-start
  6.5 8.7 %copy.13 = f32[33,2,32,256]{0,2,1,3:T(8,128)} copy(f32[33,2,32,256]{3,2,1,0:T(8,128)} %param.2) | data formatting | bytes 4325376 | tf_op args[0]
  15.2 10.1 %reshape.13 = f32[16,1,33792]{2,1,0:T(1,128)S(1)} reshape(f32[256,2,32,33]{3,2,1,0:T(8,128)} %bitcast.45) | data formatting | bytes 4325376
  25.3 34.1 %all_to_all.36 = f32[16,1,33792]{2,1,0:T(1,128)} all-to-all(f32[16,1,33792]{2,1,0:T(1,128)S(1)} %reshape.13), channel_id=1, replica_groups=mesh['fib'=16,'blk'=32] {'fib'}, dimensions={0} | all-to-all | bytes 4325376 | tf_op jit(solution)/shard_map/all_to_all | solution.py:9
  59.4 0.5 broadcast.53
  59.9 7.4 %reduce.6 = f32[16,33792]{1,0:T(8,128)S(1)} reduce(f32[16,1,33792]{2,1,0:T(1,128)} %all_to_all.36, f32[]{:T(128)} %broadcast.53), dimensions={1}, to_apply=%all_to_all.26.reduce_sub_computation | reduce | bytes 4325380 | tf_op jit(solution)/shard_map/all_to_all | solution.py:9
  67.3 12.4 %reshape.14 = f32[256,2,32,33]{3,2,1,0:T(8,128)} reshape(f32[16,33792]{1,0:T(8,128)S(1)} %reduce.6) | data formatting | bytes 4325376
  79.8 11.7 %copy.15 = f32[33,2,16,32,16]{3,2,4,1,0:T(8,128)} copy(f32[33,2,16,32,16]{0,3,1,4,2:T(8,128)} %bitcast.46) | data formatting | bytes 4325376 | tf_op jit(solution)/shard_map/all_to_all | solution.py:9
  91.5 6.7 %all_to_all.29 = f32[33,2,512,16]{2,3,1,0:T(8,128)S(1)} reshape(f32[33,2,16,32,16]{3,2,4,1,0:T(8,128)} %copy.15) | data formatting | bytes 4325376 | tf_op jit(solution)/shard_map/all_to_all | solution.py:9
  98.2 5.4 %fusion.4 = f32[512,512]{1,0:T(8,128)} fusion(f32[33,2,512,16]{2,3,1,0:T(8,128)S(1)} %all_to_all.29), kind=kOutput, calls=%fused_computation.4 | convolution fusion | flops 3321888768 | bytes 3211264 | tf_op jit(solution)/shard_map/dot_general | solution.py:13
  103.5 0.0 all-reduce.3.cloned.1.call-update
  103.6 0.0 all-reduce.5.cloned.1.call-start
  103.6 120.0 %all-reduce.3.cloned.1.call-done = f32[512,512]{1,0:T(8,128)} async-done(((f32[512,512]{1,0:T(8,128)}), f32[512,512]{1,0:T(8,128)}) %all-reduce.3.cloned.1.call-update) | async-done | bytes 1048592 | tf_op jit(solution)/shard_map/psum | solution.py:14
  223.6 0.0 all-reduce.5.cloned.1.call-update
  223.6 213.3 %all-reduce.5.cloned.1.call-done = f32[512,512]{1,0:T(8,128)} async-done(((f32[512,512]{1,0:T(8,128)}), f32[512,512]{1,0:T(8,128)}) %all-reduce.5.cloned.1.call-update) | async-done | bytes 1048592 | tf_op jit(solution)/shard_map/psum | solution.py:14
  436.9 0.0 copy-done
  436.9 2.4 fusion.13
  439.3 0.3 fusion.14
  439.6 0.1 copy.16
  439.7 5.8 %cholesky.16 = f32[64,64]{1,0:T(8,128)S(1)} custom-call(f32[64,64]{1,0:T(8,128)S(1)} %fusion.12), custom_call_target="Cholesky" | custom-call | tf_op jit(solution)/shard_map/jit(cholesky)/cholesky | solution.py:17
  445.5 0.7 compare_reduce_fusion
  446.3 0.7 fusion.10
  447.0 4.9 %custom-call.7 = f32[1,64,64]{1,2,0:T(8,128)S(1)} custom-call(f32[1,64,64]{2,1,0:T(8,128)S(1)} %fusion.10), custom_call_target="InvertDiagBlocksLowerTriangular" | custom-call | tf_op jit(solution)/shard_map/jit(_solve_triangular)/triangular_solve | solution.py:18
  451.9 0.3 convolution_bitcast_fusion
  452.2 3.0 fusion.7
  455.2 1.0 copy.18
  456.2 1.0 reshape.15
  457.3 14.5 %all_to_all.37 = f32[16,1,4224]{2,1,0:T(1,128)S(1)} all-to-all(f32[16,1,4224]{2,1,0:T(1,128)S(1)} %reshape.15), channel_id=1, replica_groups=mesh['fib'=16,'blk'=32] {'fib'}, dimensions={0} | all-to-all | bytes 540672 | tf_op jit(solution)/shard_map/all_to_all | solution.py:20
  471.8 1.3 reduce.7
  473.1 1.1 reshape.16
  474.2 0.1 copy.20
  474.4 1.0 copy.21
  (2 shorter events, 0.0 us)
Async XLA Ops:
  6.5 430.4 %copy-start = (f32[512,64]{0,1:T(8,128)S(1)}, f32[512,64]{0,1:T(8,128)}, u32[]{:S(2)}) copy-start(f32[512,64]{0,1:T(8,128)} %param.3) | copy-start | bytes 393220
  6.5 217.0 %all-reduce.3.cloned.1.call-start = ((), (), s32[]{:S(2)}) async-start(), calls=%async_computation.2 | async-start | bytes 2097152 | tf_op jit(solution)/shard_map/psum | solution.py:14
  103.6 333.4 %all-reduce.5.cloned.1.call-start = ((), (), s32[]{:S(2)}) async-start(), calls=%async_computation.3 | async-start | bytes 2097152 | tf_op jit(solution)/shard_map/psum | solution.py:14
Sparse Core Ops, SparseCore 0:
  103.7 119.8 all-reduce.2
  225.9 210.9 all-reduce.4
